TPU v7x, 32 devices: a whole 2x2x4 slice. The times are simulated.
32 devices in a mesh: row: 4 (over y, x), col: 8 (over z, core).
Axes of the slice: x: 2, y: 2, z: 4, core: 2. Of those that a mesh axis runs over, the one named last changes fastest.
Arguments:
- scalar_field: float32 [256, 256, 1024], P('col', 'row'), may hold values from -1.2 to 1.2
- reaction: float32 [256, 256, 1024], P('col', 'row'), may hold values from 0.5 to 4
- x_faces: float32 [1024], replicated, may hold values from 0.5 to 4
- y_faces: float32 [256], replicated, may hold values from 0.5 to 4
- z_faces: float32 [256], replicated, may hold values from 0.5 to 4
- x_inverse: float32 [8, 128, 128], replicated, may hold values from 0 to 1, as said below
- y_inverse: float32 [2, 128, 128], replicated, may hold values from 0 to 1, as said below
- z_inverse: float32 [2, 128, 128], replicated, may hold values from 0 to 1, as said below
Outputs:
- advanced: float32 [256, 256, 1024], P('col', 'row')
Inputs may be any that keep to these rules, and one draw needn't show every extreme that they name: x_inverse[c] is, up to float32 rounding, the inverse of the block of rows and columns c * 128 to (c + 1) * 128 - 1 of the matrix I - 500 A_x along one x line. y_inverse[c] is, up to float32 rounding, the inverse of the block of rows and columns c * 128 to (c + 1) * 128 - 1 of the matrix I - 500 A_y along one y line. z_inverse[c] is, up to float32 rounding, the inverse of the block of rows and columns c * 128 to (c + 1) * 128 - 1 of the matrix I - 500 A_z along one z line.
All inputs are finite; a program needn't handle non-finite values.
Results may differ from a plain program's by a relative error of at most 0.0003.
Values sent between devices are 32-bit elements; how exact they have to be, the bound alone decides.
A program may use at most 128 MiB of HBM per device.

v0:
```python
import jax
import jax.numpy as jnp
from jax import lax
from jax.sharding import PartitionSpec as P

implicit_weight = 0.5
time_step = 1000.0


def with_halo(shard, sides, width):
    for axis, dim in sides:
        size, length = (lax.axis_size(axis), shard.shape[dim])
        up = [(i, (i + 1) % size) for i in range(size - 1)]
        down = [(j, i) for i, j in up]
        last = lax.slice_in_dim(shard, length - width, length, axis=dim)
        leading = lax.slice_in_dim(shard, 0, width, axis=dim)
        before = lax.ppermute(last, axis, up)
        after = lax.ppermute(leading, axis, down)
        shard = jnp.concatenate([before, shard, after], axis=dim)
    return shard


def shift_lower(values, line_axis):
    length = values.shape[line_axis]
    first_slot = jnp.zeros_like(lax.slice_in_dim(values, 0, 1, axis=line_axis))
    return jnp.concatenate(
        [first_slot, lax.slice_in_dim(values, 0, length - 1, axis=line_axis)], axis=line_axis
    )


def shift_upper(values, line_axis):
    length = values.shape[line_axis]
    last_slot = jnp.zeros_like(lax.slice_in_dim(values, 0, 1, axis=line_axis))
    return jnp.concatenate(
        [lax.slice_in_dim(values, 1, length, axis=line_axis), last_slot], axis=line_axis
    )


def apply_line(values, face_values, line_axis):
    spread = [1, 1, 1]
    spread[line_axis] = values.shape[line_axis]
    face_here = face_values.reshape(spread)
    face_next = jnp.concatenate([face_values[1:], jnp.zeros((1,), face_values.dtype)]).reshape(
        spread
    )
    lower_value = shift_lower(values, line_axis)
    upper_value = shift_upper(values, line_axis)
    return face_next * (upper_value - values) - face_here * (values - lower_value)


def invert_small(matrix):
    order = matrix.shape[0]
    joined = jnp.concatenate([matrix, jnp.eye(order, dtype=matrix.dtype)], axis=1)

    def sweep(step_index, current):
        pivot_row = lax.dynamic_index_in_dim(current, step_index, 0, keepdims=False)
        pivot_row = pivot_row / lax.dynamic_index_in_dim(pivot_row, step_index, 0, keepdims=False)
        pivot_column = lax.dynamic_slice_in_dim(current, step_index, 1, 1)
        current = current - pivot_column * pivot_row[None, :]
        return lax.dynamic_update_index_in_dim(current, pivot_row, step_index, 0)

    joined = lax.fori_loop(0, order, sweep, joined)
    return joined[:, order:]


def reduced_inverse(inverse, coupling_before, coupling_after):
    groups, block_width = (inverse.shape[0], inverse.shape[1])
    order = 2 * groups
    group_index = jnp.arange(groups)
    lead_rows = 2 * group_index
    trail_rows = 2 * group_index + 1
    prev_cols = jnp.maximum(2 * group_index - 1, 0)
    next_cols = jnp.minimum(2 * group_index + 2, order - 1)
    coupled = jnp.zeros((order, order), inverse.dtype)
    coupled = coupled.at[lead_rows, prev_cols].add(coupling_before * inverse[:, 0, 0])
    coupled = coupled.at[lead_rows, next_cols].add(coupling_after * inverse[:, 0, block_width - 1])
    coupled = coupled.at[trail_rows, prev_cols].add(
        coupling_before * inverse[:, block_width - 1, 0]
    )
    coupled = coupled.at[trail_rows, next_cols].add(
        coupling_after * inverse[:, block_width - 1, block_width - 1]
    )
    return invert_small(jnp.eye(order, dtype=inverse.dtype) - coupled)


def line_solve(right_side, inverse, face_values, line_axis):
    groups, block_width = (inverse.shape[0], inverse.shape[1])
    dims_full = right_side.shape
    blocked = right_side.reshape(
        dims_full[:line_axis] + (groups, block_width) + dims_full[line_axis + 1 :]
    )
    others = ["u", "v"]
    source = "".join(others[:line_axis] + ["c", "j"] + others[line_axis:])
    target = "".join(others[:line_axis] + ["c", "i"] + others[line_axis:])
    inside = jnp.einsum(
        "cij," + source + "->" + target, inverse, blocked, precision=lax.Precision.HIGHEST
    )
    leading = lax.index_in_dim(inside, 0, line_axis + 1, keepdims=False)
    trailing = lax.index_in_dim(inside, block_width - 1, line_axis + 1, keepdims=False)
    coupling = implicit_weight * time_step * face_values[block_width::block_width]
    nothing = jnp.zeros((1,), face_values.dtype)
    coupling_before = jnp.concatenate([nothing, coupling])
    coupling_after = jnp.concatenate([coupling, nothing])
    reduced = reduced_inverse(inverse, coupling_before, coupling_after)
    interface = jnp.stack([leading, trailing], axis=line_axis + 1)
    interface = interface.reshape(
        dims_full[:line_axis] + (2 * groups,) + dims_full[line_axis + 1 :]
    )
    end_source = "".join(others[:line_axis] + ["j"] + others[line_axis:])
    end_target = "".join(others[:line_axis] + ["i"] + others[line_axis:])
    solved = jnp.einsum(
        "ij," + end_source + "->" + end_target, reduced, interface, precision=lax.Precision.HIGHEST
    )
    solved = solved.reshape(dims_full[:line_axis] + (groups, 2) + dims_full[line_axis + 1 :])
    first_values = lax.index_in_dim(solved, 0, line_axis + 1, keepdims=False)
    last_values = lax.index_in_dim(solved, 1, line_axis + 1, keepdims=False)
    prev_last = shift_lower(last_values, line_axis)
    next_first = shift_upper(first_values, line_axis)
    spike_shape = [1, 1, 1, 1]
    spike_shape[line_axis] = groups
    spike_shape[line_axis + 1] = block_width
    left_spike = (coupling_before[:, None] * inverse[:, :, 0]).reshape(spike_shape)
    right_spike = (coupling_after[:, None] * inverse[:, :, block_width - 1]).reshape(spike_shape)
    result = (
        inside
        + left_spike * jnp.expand_dims(prev_last, line_axis + 1)
        + right_spike * jnp.expand_dims(next_first, line_axis + 1)
    )
    return result.reshape(dims_full)


def body(scalar_field, reaction, x_faces, y_faces, z_faces, x_inverse, y_inverse, z_inverse):
    z_cells, y_cells, x_cells = scalar_field.shape
    padded = with_halo(scalar_field, (("row", 1), ("col", 0)), 1)
    nothing = jnp.zeros((1,), jnp.float32)
    y_padded = jnp.concatenate([y_faces, nothing])
    z_padded = jnp.concatenate([z_faces, nothing])
    y_start = lax.axis_index("row") * y_cells
    z_start = lax.axis_index("col") * z_cells
    y_here = lax.dynamic_slice_in_dim(y_padded, y_start, y_cells).reshape(1, y_cells, 1)
    y_next = lax.dynamic_slice_in_dim(y_padded, y_start + 1, y_cells).reshape(1, y_cells, 1)
    z_here = lax.dynamic_slice_in_dim(z_padded, z_start, z_cells).reshape(z_cells, 1, 1)
    z_next = lax.dynamic_slice_in_dim(z_padded, z_start + 1, z_cells).reshape(z_cells, 1, 1)
    y_term = y_next * (padded[1:-1, 2:, :] - scalar_field) - y_here * (
        scalar_field - padded[1:-1, :-2, :]
    )
    z_term = z_next * (padded[2:, 1:-1, :] - scalar_field) - z_here * (
        scalar_field - padded[:-2, 1:-1, :]
    )
    x_term = apply_line(scalar_field, x_faces, 2)
    source = reaction * scalar_field * (1.0 - scalar_field * scalar_field)
    change = time_step * (x_term + y_term + z_term + source)
    first_section = line_solve(change, x_inverse, x_faces, 2)
    section_y = lax.all_to_all(first_section, "row", split_axis=2, concat_axis=1, tiled=True)
    second_section = line_solve(section_y, y_inverse, y_faces, 1)
    section_z = lax.all_to_all(second_section, "col", split_axis=1, concat_axis=0, tiled=True)
    total_change = line_solve(section_z, z_inverse, z_faces, 0)
    returned = lax.all_to_all(
        lax.all_to_all(total_change, "col", split_axis=0, concat_axis=1, tiled=True),
        "row",
        split_axis=1,
        concat_axis=2,
        tiled=True,
    )
    return scalar_field + returned


def solution(mesh):
    in_specs = (P("col", "row", None), P("col", "row", None), P(), P(), P(), P(), P(), P())
    out_specs = P("col", "row", None)
    return jax.shard_map(body, mesh=mesh, in_specs=in_specs, out_specs=out_specs, check_vma=False)
```

profile of v0, /device:TPU:0, one launch (start us, length us, event | category | flops | bytes accessed | tf_op | source)
XLA Modules:
  0.0 899.9 jit_solution(2791366461174702454)
XLA Ops:
  3.1 5.5 collective-permute-start.1
  8.7 13.3 %fusion.72 = (f32[32,64,1023]{2,1,0:T(8,128)}, f32[32,64,1023]{2,1,0:T(8,128)}) fusion(f32[32,64,1024]{2,1,0:T(8,128)} %param.14), kind=kLoop, calls=%fused_computation.182 | loop fusion | bytes 33521664 | tf_op jit(solution)/shard_map/slice | solution.py:35
  26.2 32.5 %while.39 = (s32[]{:T(128)}, f32[16,32]{1,0:T(8,128)S(1)}, s32[]{:T(128)}, s32[]{:T(128)}, s32[]{:T(128)}, /*index=5*/s32[]{:T(128)}) while((s32[]{:T(128)}, f32[16,32]{1,0:T(8,128)S(1)}, s32[]{:T(128)}, s32[]{:T(128)}, s32[]{:T(128)}, /*index=5*/s32[]{:T(128)}) %tuple.111), condition=%wide.region_5.6_spmd, body=%wide.region_4.5_spmd.sunk | while | flops 1092 | bytes 5321 | solution.py:62
  66.0 28.5 %fusion.22 = f32[32,64,8,128]{3,1,0,2:T(8,128)S(1)} fusion(f32[8,128,128]{2,1,0:T(8,128)S(1)} %copy-done.2, f32[32,64,1024]{2,1,0:T(8,128)} %param.14, f32[1,66,1024]{2,1,0:T(8,128)S(1)} %collective-permute-done.3, f32[32,1,1024]{2,1,0:T(1,128)S(1)} %copy.140, f32[32,1,1024]{2,1,0:T(1,128)S(1)} %copy.142, f32[1,66,1024]{2,1,0:T(8,128)S(1)} %collective-permute-done.2, ...), kind=kOutput, calls=%fused_computation.55 | convolution fusion | flops 3286237184 | bytes 43262720 | tf_op jit(solution)/shard_map/cij,uvcj->uvci/dot_general | solution.py:95
  94.4 7.9 fusion.71
  102.9 11.9 %pad_maximum_fusion.8 = f32[32,64,8,2]{3,1,0,2:T(8,128)} fusion(f32[32,64,8,1]{3,1,0,2:T(8,128)} %get-tuple-element.190, f32[32,64,8,1]{3,1,0,2:T(8,128)} %get-tuple-element.189), kind=kLoop, calls=%fused_computation.47 | loop fusion | flops 32768 | bytes 262144 | tf_op jit(solution)/shard_map/stack | solution.py:105
  114.8 5.4 copy.147
  120.9 10.5 %multiply_add_fusion.2 = f32[32,64,8,128]{3,1,0,2:T(8,128)} fusion(f32[32,64,8,128]{3,1,0,2:T(8,128)} %copy-done, f32[32,64,8]{1,0,2:T(8,128)S(1)} %concatenate.122.clone, f32[8,128]{1,0:T(8,128)S(1)} %get-tuple-element.229, f32[32,64,8]{1,0,2:T(8,128)S(1)} %concatenate.121.clone, f32[8,128]{1,0:T(8,128)S(1)} %get-tuple-element.230), kind=kLoop, calls=%fused_computation.54 | loop fusion | flops 8388608 | bytes 16916480 | tf_op jit(solution)/shard_map/add | solution.py:125
  131.4 16.2 %copy.183 = f32[32,64,8,128]{1,0,3,2:T(8,128)} copy(f32[32,64,8,128]{3,1,0,2:T(8,128)} %multiply_add_fusion.2) | data formatting | bytes 16777216 | tf_op jit(solution)/shard_map/reshape | solution.py:129
  147.6 14.7 %reshape.391 = f32[4,1,524288]{2,1,0:T(1,128)} reshape(f32[1024,32,64]{2,1,0:T(8,128)} %bitcast.128) | data formatting | bytes 16777216
  162.3 5.8 all-to-all-start
  176.8 8.8 while.40
  185.5 75.3 %all-to-all-done = f32[4,1,524288]{2,1,0:T(1,128)} async-done(((f32[4,1,524288]{2,1,0:T(1,128)}), f32[4,1,524288]{2,1,0:T(1,128)}, u32[]{:S(2)}, u32[]{:S(2)}) %all-to-all-start) | async-done | bytes 8388640 | tf_op jit(solution)/shard_map/all_to_all | solution.py:154
  261.3 28.3 %reduce.38 = f32[4,524288]{1,0:T(4,128)} reduce(f32[4,1,524288]{2,1,0:T(1,128)} %all-to-all-done, f32[]{:T(128)} %broadcast.1002), dimensions={1}, to_apply=%all_to_all.48.reduce_sub_computation | reduce | bytes 16777220 | tf_op jit(solution)/shard_map/all_to_all | solution.py:154
  289.7 16.8 %reshape.392 = f32[1024,32,64]{2,1,0:T(8,128)} reshape(f32[4,524288]{1,0:T(4,128)} %reduce.38) | data formatting | bytes 16777216
  306.4 13.0 %copy.184 = f32[32,64,4,256]{3,2,1,0:T(4,128)} copy(f32[32,64,4,256]{1,0,3,2:T(8,128)} %bitcast.129) | data formatting | bytes 16777216 | tf_op jit(solution)/shard_map/all_to_all | solution.py:154
  319.4 5.0 copy.156
  324.4 8.6 fusion.25
  337.5 5.4 multiply_add_fusion.1
  344.2 8.3 copy.163
  352.5 8.6 all-to-all-start.1
  361.1 8.1 while.41
  369.7 175.4 %all-to-all-done.1 = f32[32,256,256]{2,0,1:T(8,128)} async-done(((f32[32,256,256]{2,0,1:T(8,128)}), f32[32,256,256]{2,0,1:T(8,128)}, u32[]{:S(2)}, u32[]{:S(2)}) %all-to-all-start.1) | async-done | bytes 8388640 | tf_op jit(solution)/shard_map/all_to_all | solution.py:156
  545.1 8.2 copy.165
  553.3 13.4 %fusion.28 = f32[2,128,32,256]{3,1,2,0:T(8,128)S(1)} fusion(f32[2,128,32,256]{3,2,1,0:T(8,128)S(1)} %bitcast.133, f32[2,128,128]{2,1,0:T(8,128)S(1)} %copy-done.4), kind=kOutput, calls=%fused_computation.57 | convolution fusion | flops 3221225472 | bytes 16908288 | tf_op jit(solution)/shard_map/cij,cjuv->ciuv/dot_general | solution.py:95
  569.9 5.1 copy.171
  574.9 186.4 %all_to_all.66 = f32[256,32,256]{2,1,0:T(8,128)S(1)} all-to-all(f32[256,32,256]{2,1,0:T(8,128)S(1)} %bitcast.134), channel_id=1, replica_groups=mesh['row'=4,'col'=8] {'col'}, dimensions={0} | all-to-all | bytes 16777216 | tf_op jit(solution)/shard_map/all_to_all | solution.py:159
  763.0 4.9 copy.173
  767.9 96.7 %all_to_all.67 = f32[32,256,256]{2,0,1:T(8,128)} all-to-all(f32[32,256,256]{2,0,1:T(8,128)S(1)} %copy.173), channel_id=1, replica_groups=mesh['row'=4,'col'=8] {'row'}, dimensions={1} | all-to-all | bytes 16777216 | tf_op jit(solution)/shard_map/all_to_all | solution.py:158
  864.6 12.2 %copy.175 = f32[32,64,4,256]{3,2,1,0:T(4,128)} copy(f32[32,64,4,256]{3,0,1,2:T(8,128)} %bitcast.137) | data formatting | bytes 16777216 | tf_op jit(solution)/shard_map/all_to_all | solution.py:158
  876.8 10.7 %all_to_all.61 = f32[32,64,1024]{2,1,0:T(8,128)} reshape(f32[32,64,4,256]{3,2,1,0:T(4,128)} %copy.175) | data formatting | bytes 16777216 | tf_op jit(solution)/shard_map/all_to_all | solution.py:158
  887.5 12.1 %add.391 = f32[32,64,1024]{2,1,0:T(8,128)} add(f32[32,64,1024]{2,1,0:T(8,128)} %param.14, f32[32,64,1024]{2,1,0:T(8,128)} %all_to_all.61) | non-fusion elementwise | flops 2097152 | bytes 25165824 | tf_op jit(solution)/shard_map/add | solution.py:165
  (266 shorter events, 83.1 us)
Async XLA Ops:
  1.8 57.2 %collective-permute-start = (f32[32,1,1024]{2,0,1:T(8,128)S(1)}, f32[32,1,1024]{2,0,1:T(8,128)S(1)}, u32[]{:S(2)}, u32[]{:S(2)}) collective-permute-start(f32[32,1,1024]{2,0,1:T(8,128)S(1)} %copy.188), channel_id=1, source_target_pairs={{8,0},{16,8},{24,16},{9,1},{17,9},{25,17},{10,2},{18,10},{26,18},{... | collective-permute-start | bytes 393224 | tf_op jit(solution)/shard_map/ppermute | solution.py:18
  3.1 56.0 %collective-permute-start.1 = (f32[32,1,1024]{2,0,1:T(8,128)S(1)}, f32[32,1,1024]{2,0,1:T(8,128)S(1)}, u32[]{:S(2)}, u32[]{:S(2)}) collective-permute-start(f32[32,1,1024]{2,0,1:T(8,128)S(1)} %copy.189), channel_id=1, source_target_pairs={{0,8},{8,16},{16,24},{1,9},{9,17},{17,25},{2,10},{10,18},{18,26},{... | collective-permute-start | bytes 393224 | tf_op jit(solution)/shard_map/ppermute | solution.py:17
  8.7 13.4 %copy-start.2 = (f32[8,128,128]{2,1,0:T(8,128)S(1)}, f32[8,128,128]{2,1,0:T(8,128)}, u32[]{:S(2)}) copy-start(f32[8,128,128]{2,1,0:T(8,128)} %param.19) | copy-start | bytes 1572868
  8.7 13.8 %copy-start.5 = (f32[1024]{0:T(1024)S(1)}, f32[1024]{0:T(1024)}, u32[]{:S(2)}) copy-start(f32[1024]{0:T(1024)} %param.16) | copy-start | bytes 12292
  8.7 50.1 %copy-start.6 = (f32[256]{0:T(256)S(1)}, f32[256]{0:T(256)}, u32[]{:S(2)}) copy-start(f32[256]{0:T(256)} %param.18) | copy-start | bytes 3076
  8.7 50.1 %copy-start.7 = (f32[256]{0:T(256)S(1)}, f32[256]{0:T(256)}, u32[]{:S(2)}) copy-start(f32[256]{0:T(256)} %param.17) | copy-start | bytes 3076
  60.4 5.1 collective-permute-start.2
  61.7 4.2 collective-permute-start.3
  94.4 8.4 copy-start
  162.3 8.1 copy-start.4
  162.3 9.0 copy-start.3
  162.3 98.6 %all-to-all-start = ((f32[4,1,524288]{2,1,0:T(1,128)}), f32[4,1,524288]{2,1,0:T(1,128)}, u32[]{:S(2)}, u32[]{:S(2)}) async-start(f32[4,1,524288]{2,1,0:T(1,128)} %reshape.391), calls=%async_computation | async-start | bytes 16777216 | tf_op jit(solution)/shard_map/all_to_all | solution.py:154
  333.1 3.4 copy-start.1
  352.5 192.6 %all-to-all-start.1 = ((f32[32,256,256]{2,0,1:T(8,128)}), f32[32,256,256]{2,0,1:T(8,128)}, u32[]{:S(2)}, u32[]{:S(2)}) async-start(f32[32,256,256]{2,0,1:T(8,128)} %copy.163), calls=%async_computation.1 | async-start | bytes 16777216 | tf_op jit(solution)/shard_map/all_to_all | solution.py:156
where the time goes:
time: 905 us; the launch traced here: 900 us
  blocking collectives  283 us (31%)
  waiting for transfers between devices  251 us (28%)
  local copies, waits for them, and re-layouts  174 us (19%)
  other arithmetic  112 us (12%)
  matrix products  51.9 us (6%)
  starting transfers between devices  25.8 us (3%)
    all_to_all x1, blocking collectives, body(): lax.all_to_all(total_change, 'col', split_axis=0, concat_axis=1, tiled=True)  186 us
    all_to_all x1, waiting for transfers between devices, body(): lax.all_to_all(second_section, 'col', split_axis=1, concat_axis=0, tiled=...  175 us
    all_to_all x1, blocking collectives, body(): lax.all_to_all(lax.all_to_all(total_change, 'col', split_axis=0, concat_a...  96.7 us
    all_to_all x1, waiting for transfers between devices, body(): lax.all_to_all(first_section, 'row', split_axis=2, concat_axis=1, tiled=T...  75.3 us
    dot_general x3, matrix products, line_solve(): jnp.einsum('cij,' + source + '->' + target, inverse, blocked, precision=l...  50.5 us
    unnamed x28, local copies, waits for them, and re-layouts  35.9 us
    all_to_all x1, other arithmetic, body(): lax.all_to_all(first_section, 'row', split_axis=2, concat_axis=1, tiled=T...  28.3 us
    reshape x2, local copies, waits for them, and re-layouts, line_solve(): return result.reshape(dims_full)  24.5 us
  transfers between devices with their start and end apart: 6, of which 3 were waited for; matrix products, arithmetic and copies ran while one was open for 8% of the time, Pallas kernels for 0%

commit v1 on v0

--- a/solution.py
+++ b/solution.py
@@ -151,7 +151,12 @@
     source = reaction * scalar_field * (1.0 - scalar_field * scalar_field)
     change = time_step * (x_term + y_term + z_term + source)
     first_section = line_solve(change, x_inverse, x_faces, 2)
-    section_y = lax.all_to_all(first_section, "row", split_axis=2, concat_axis=1, tiled=True)
+    section_y = jnp.concatenate(
+        lax.all_to_all(
+            jnp.stack(jnp.split(first_section, lax.axis_size("row"), axis=2)), "row", 0, 0
+        ),
+        axis=1,
+    )
     second_section = line_solve(section_y, y_inverse, y_faces, 1)
     section_z = lax.all_to_all(second_section, "col", split_axis=1, concat_axis=0, tiled=True)
     total_change = line_solve(section_z, z_inverse, z_faces, 0)

time: 905 us -> 817 us (0.903)
  local copies, waits for them, and re-layouts: 174 us -> 113 us
  other arithmetic: 112 us -> 84.7 us
    unnamed x28 -> x26, local copies, waits for them, and re-layouts: 35.9 us -> 4.47 us
    all_to_all x1 -> x0, other arithmetic: 28.3 us -> none  [body(): lax.all_to_all(first_section, 'row', split_axis=2, concat_axis=1, tiled=T...]
    all_to_all x3 -> x0, local copies, waits for them, and re-layouts: 18.5 us -> none  [body(): lax.all_to_all(first_section, 'row', split_axis=2, concat_axis=1, tiled=T...]
    reshape x2 -> x1, local copies, waits for them, and re-layouts: 24.5 us -> 8.66 us  [line_solve(): return result.reshape(dims_full)]
    add x3 -> x2, other arithmetic: 18.2 us -> 7.66 us  [line_solve(): inside + left_spike * jnp.expand_dims(prev_last, line_axis + 1)]
  transfers between devices with their start and end apart: 6 -> 6, of which waited for: 3 -> 2; matrix products, arithmetic and copies ran while one was open for 8% -> 9% of each run, Pallas kernels for 0% -> 0%
where the time goes in v1:
time: 817 us; the launch traced here: 812 us
  blocking collectives  283 us (35%)
  waiting for transfers between devices  251 us (31%)
  local copies, waits for them, and re-layouts  113 us (14%)
  other arithmetic  84.7 us (10%)
  matrix products  51.9 us (6%)
  starting transfers between devices  26.1 us (3%)
    all_to_all x1, blocking collectives, body(): lax.all_to_all(total_change, 'col', split_axis=0, concat_axis=1, tiled=True)  186 us
    all_to_all x1, waiting for transfers between devices, body(): lax.all_to_all(second_section, 'col', split_axis=1, concat_axis=0, tiled=...  175 us
    all_to_all x1, blocking collectives, body(): lax.all_to_all(lax.all_to_all(total_change, 'col', split_axis=0, concat_a...  96.7 us
    all_to_all x1, waiting for transfers between devices, body(): lax.all_to_all(jnp.stack(jnp.split(first_section, lax.axis_size('row'), a...  75.2 us
    dot_general x3, matrix products, line_solve(): jnp.einsum('cij,' + source + '->' + target, inverse, blocked, precision=l...  50.5 us
    all_to_all x2, local copies, waits for them, and re-layouts, body(): lax.all_to_all(lax.all_to_all(total_change, 'col', split_axis=0, concat_a...  22.9 us
  transfers between devices with their start and end apart: 6, of which 2 were waited for; matrix products, arithmetic and copies ran while one was open for 9% of the time, Pallas kernels for 0%

profile of v1, /device:TPU:0, one launch (start us, length us, event | category | flops | bytes accessed | tf_op | source)
XLA Modules:
  0.0 812.1 jit_solution(12161690091487228929)
XLA Ops:
  0.0 1.8 fusion.73
  3.1 5.5 collective-permute-start.1
  8.7 13.3 %fusion.72 = (f32[32,64,1023]{2,1,0:T(8,128)}, f32[32,64,1023]{2,1,0:T(8,128)}) fusion(f32[32,64,1024]{2,1,0:T(8,128)} %param.14), kind=kLoop, calls=%fused_computation.188 | loop fusion | bytes 33521664 | tf_op jit(solution)/shard_map/slice | solution.py:35
  26.2 32.5 %while.39 = (s32[]{:T(128)}, f32[16,32]{1,0:T(8,128)S(1)}, s32[]{:T(128)}, s32[]{:T(128)}, s32[]{:T(128)}, /*index=5*/s32[]{:T(128)}) while((s32[]{:T(128)}, f32[16,32]{1,0:T(8,128)S(1)}, s32[]{:T(128)}, s32[]{:T(128)}, s32[]{:T(128)}, /*index=5*/s32[]{:T(128)}) %tuple.114), condition=%wide.region_5.6_spmd, body=%wide.region_4.5_spmd.sunk | while | flops 1092 | bytes 5321 | solution.py:62
  61.7 3.6 collective-permute-start.3
  66.0 28.5 %fusion.22 = f32[32,64,8,128]{3,1,0,2:T(8,128)S(1)} fusion(f32[8,128,128]{2,1,0:T(8,128)S(1)} %copy-done.2, f32[32,64,1024]{2,1,0:T(8,128)} %param.14, f32[1,66,1024]{2,1,0:T(8,128)S(1)} %collective-permute-done.3, f32[32,1,1024]{2,1,0:T(1,128)S(1)} %copy.138, f32[32,1,1024]{2,1,0:T(1,128)S(1)} %copy.140, f32[1,66,1024]{2,1,0:T(8,128)S(1)} %collective-permute-done.2, ...), kind=kOutput, calls=%fused_computation.57 | convolution fusion | flops 3286237184 | bytes 43262720 | tf_op jit(solution)/shard_map/cij,uvcj->uvci/dot_general | solution.py:95
  94.4 7.9 fusion.71
  102.9 11.9 %pad_maximum_fusion.8 = f32[32,64,8,2]{3,1,0,2:T(8,128)} fusion(f32[32,64,8,1]{3,1,0,2:T(8,128)} %get-tuple-element.194, f32[32,64,8,1]{3,1,0,2:T(8,128)} %get-tuple-element.193), kind=kLoop, calls=%fused_computation.48 | loop fusion | flops 32768 | bytes 262144 | tf_op jit(solution)/shard_map/stack | solution.py:105
  114.8 5.4 copy.145
  120.9 8.2 %copy_bitcast_fusion = f32[32,64,1024]{2,1,0:T(8,128)S(1)} fusion(f32[32,64,8,128]{3,1,0,2:T(8,128)} %copy-done, f32[32,64,8]{1,0,2:T(8,128)S(1)} %concatenate.122.clone, f32[8,128]{1,0:T(8,128)S(1)} %get-tuple-element.233, f32[32,64,8]{1,0,2:T(8,128)S(1)} %concatenate.121.clone, f32[8,128]{1,0:T(8,128)S(1)} %get-tuple-element.234), kind=kLoop, calls=%fused_computation.21 | loop fusion | flops 8388608 | bytes 16916480 | tf_op jit(solution)/shard_map/reshape | solution.py:129
  130.4 3.7 pad_maximum_fusion.9
  134.0 5.8 all-to-all-start
  148.5 8.9 %while.40 = (s32[]{:T(128)}, f32[4,8]{1,0:T(4,128)S(1)}, s32[]{:T(128)}, s32[]{:T(128)}, s32[]{:T(128)}, /*index=5*/s32[]{:T(128)}) while((s32[]{:T(128)}, f32[4,8]{1,0:T(4,128)S(1)}, s32[]{:T(128)}, s32[]{:T(128)}, s32[]{:T(128)}, /*index=5*/s32[]{:T(128)}) %tuple.117), condition=%wide.region_11.12_spmd, body=%wide.region_10.11_spmd.sunk | while | flops 84 | bytes 665 | solution.py:62
  157.4 75.2 %all-to-all-done = f32[4,32,64,256]{3,2,1,0:T(8,128)} async-done(((f32[4,32,64,256]{3,2,1,0:T(8,128)}), f32[4,32,64,256]{3,2,1,0:T(8,128)}, u32[]{:S(2)}, u32[]{:S(2)}) %all-to-all-start) | async-done | bytes 8388640 | tf_op jit(solution)/shard_map/all_to_all | solution.py:155
  232.6 4.0 copy.152
  236.6 8.6 %fusion.25 = f32[32,2,128,256]{3,2,0,1:T(8,128)S(1)} fusion(f32[32,2,128,256]{3,2,1,0:T(8,128)S(1)} %bitcast.137, f32[2,128,128]{2,1,0:T(8,128)S(1)} %copy-done.3), kind=kOutput, calls=%fused_computation.58 | convolution fusion | flops 3221225472 | bytes 16908288 | tf_op jit(solution)/shard_map/cij,ucjv->uciv/dot_general | solution.py:95
  245.2 3.4 copy-done.1
  249.6 5.4 multiply_add_fusion.1
  256.0 8.7 %copy.159 = f32[32,256,256]{2,0,1:T(8,128)} copy(f32[32,256,256]{2,1,0:T(8,128)S(1)} %bitcast.138) | data formatting | bytes 16777216 | tf_op jit(solution)/shard_map/reshape | solution.py:129
  264.7 8.7 %all-to-all-start.1 = ((f32[32,256,256]{2,0,1:T(8,128)}), f32[32,256,256]{2,0,1:T(8,128)}, u32[]{:S(2)}, u32[]{:S(2)}) async-start(f32[32,256,256]{2,0,1:T(8,128)} %copy.159), calls=%async_computation.1 | async-start | bytes 16777216 | tf_op jit(solution)/shard_map/all_to_all | solution.py:161
  273.3 8.1 %while.41 = (s32[]{:T(128)}, f32[4,8]{1,0:T(4,128)S(1)}, s32[]{:T(128)}, s32[]{:T(128)}, s32[]{:T(128)}, /*index=5*/s32[]{:T(128)}) while((s32[]{:T(128)}, f32[4,8]{1,0:T(4,128)S(1)}, s32[]{:T(128)}, s32[]{:T(128)}, s32[]{:T(128)}, /*index=5*/s32[]{:T(128)}) %tuple.120), condition=%wide.region_17.18_spmd, body=%wide.region_16.17_spmd.sunk | while | flops 84 | bytes 665 | solution.py:62
  281.9 175.4 %all-to-all-done.1 = f32[32,256,256]{2,0,1:T(8,128)} async-done(((f32[32,256,256]{2,0,1:T(8,128)}), f32[32,256,256]{2,0,1:T(8,128)}, u32[]{:S(2)}, u32[]{:S(2)}) %all-to-all-start.1) | async-done | bytes 8388640 | tf_op jit(solution)/shard_map/all_to_all | solution.py:161
  457.3 8.2 %copy.161 = f32[8,32,32,256]{3,2,1,0:T(8,128)S(1)} copy(f32[8,32,32,256]{3,1,2,0:T(8,128)} %bitcast.42) | data formatting | bytes 16777216 | tf_op jit(solution)/shard_map/all_to_all | solution.py:161
  465.5 13.4 %fusion.28 = f32[2,128,32,256]{3,1,2,0:T(8,128)S(1)} fusion(f32[2,128,32,256]{3,2,1,0:T(8,128)S(1)} %bitcast.139, f32[2,128,128]{2,1,0:T(8,128)S(1)} %copy-done.4), kind=kOutput, calls=%fused_computation.59 | convolution fusion | flops 3221225472 | bytes 16908288 | tf_op jit(solution)/shard_map/cij,cjuv->ciuv/dot_general | solution.py:95
  479.8 2.3 multiply_add_fusion
  482.1 5.1 copy.167
  487.1 186.4 %all_to_all.56 = f32[256,32,256]{2,1,0:T(8,128)S(1)} all-to-all(f32[256,32,256]{2,1,0:T(8,128)S(1)} %bitcast.140), channel_id=1, replica_groups=mesh['row'=4,'col'=8] {'col'}, dimensions={0} | all-to-all | bytes 16777216 | tf_op jit(solution)/shard_map/all_to_all | solution.py:164
  675.2 4.9 copy.169
  680.1 96.7 %all_to_all.57 = f32[32,256,256]{2,0,1:T(8,128)} all-to-all(f32[32,256,256]{2,0,1:T(8,128)S(1)} %copy.169), channel_id=1, replica_groups=mesh['row'=4,'col'=8] {'row'}, dimensions={1} | all-to-all | bytes 16777216 | tf_op jit(solution)/shard_map/all_to_all | solution.py:163
  776.8 12.2 %copy.171 = f32[32,64,4,256]{3,2,1,0:T(4,128)} copy(f32[32,64,4,256]{3,0,1,2:T(8,128)} %bitcast.143) | data formatting | bytes 16777216 | tf_op jit(solution)/shard_map/all_to_all | solution.py:163
  789.0 10.7 %all_to_all.51 = f32[32,64,1024]{2,1,0:T(8,128)} reshape(f32[32,64,4,256]{3,2,1,0:T(4,128)} %copy.171) | data formatting | bytes 16777216 | tf_op jit(solution)/shard_map/all_to_all | solution.py:163
  799.7 12.1 %add.391 = f32[32,64,1024]{2,1,0:T(8,128)} add(f32[32,64,1024]{2,1,0:T(8,128)} %param.14, f32[32,64,1024]{2,1,0:T(8,128)} %all_to_all.51) | non-fusion elementwise | flops 2097152 | bytes 25165824 | tf_op jit(solution)/shard_map/add | solution.py:170
  (262 shorter events, 72.5 us)
Async XLA Ops:
  1.8 57.2 %collective-permute-start = (f32[32,1,1024]{2,0,1:T(8,128)S(1)}, f32[32,1,1024]{2,0,1:T(8,128)S(1)}, u32[]{:S(2)}, u32[]{:S(2)}) collective-permute-start(f32[32,1,1024]{2,0,1:T(8,128)S(1)} %copy.181), channel_id=1, source_target_pairs={{8,0},{16,8},{24,16},{9,1},{17,9},{25,17},{10,2},{18,10},{26,18},{... | collective-permute-start | bytes 393224 | tf_op jit(solution)/shard_map/ppermute | solution.py:18
  3.1 56.0 %collective-permute-start.1 = (f32[32,1,1024]{2,0,1:T(8,128)S(1)}, f32[32,1,1024]{2,0,1:T(8,128)S(1)}, u32[]{:S(2)}, u32[]{:S(2)}) collective-permute-start(f32[32,1,1024]{2,0,1:T(8,128)S(1)} %copy.182), channel_id=1, source_target_pairs={{0,8},{8,16},{16,24},{1,9},{9,17},{17,25},{2,10},{10,18},{18,26},{... | collective-permute-start | bytes 393224 | tf_op jit(solution)/shard_map/ppermute | solution.py:17
  8.7 13.4 %copy-start.2 = (f32[8,128,128]{2,1,0:T(8,128)S(1)}, f32[8,128,128]{2,1,0:T(8,128)}, u32[]{:S(2)}) copy-start(f32[8,128,128]{2,1,0:T(8,128)} %param.19) | copy-start | bytes 1572868
  8.7 13.8 %copy-start.5 = (f32[1024]{0:T(1024)S(1)}, f32[1024]{0:T(1024)}, u32[]{:S(2)}) copy-start(f32[1024]{0:T(1024)} %param.16) | copy-start | bytes 12292
  8.7 50.1 %copy-start.6 = (f32[256]{0:T(256)S(1)}, f32[256]{0:T(256)}, u32[]{:S(2)}) copy-start(f32[256]{0:T(256)} %param.18) | copy-start | bytes 3076
  8.7 50.1 %copy-start.7 = (f32[256]{0:T(256)S(1)}, f32[256]{0:T(256)}, u32[]{:S(2)}) copy-start(f32[256]{0:T(256)} %param.17) | copy-start | bytes 3076
  60.4 5.5 collective-permute-start.2
  61.7 4.2 collective-permute-start.3
  94.4 8.4 %copy-start = (f32[32,64,8,128]{3,1,0,2:T(8,128)}, f32[32,64,8,128]{3,1,0,2:T(8,128)S(1)}, u32[]{:S(2)}) copy-start(f32[32,64,8,128]{3,1,0,2:T(8,128)S(1)} %fusion.22) | copy-start | bytes 25165828
  134.0 8.1 copy-start.4
  134.0 9.0 %copy-start.3 = (f32[2,128,128]{2,1,0:T(8,128)S(1)}, f32[2,128,128]{2,1,0:T(8,128)}, u32[]{:S(2)}) copy-start(f32[2,128,128]{2,1,0:T(8,128)} %param.20) | copy-start | bytes 393220
  134.0 98.6 %all-to-all-start = ((f32[4,32,64,256]{3,2,1,0:T(8,128)}), f32[4,32,64,256]{3,2,1,0:T(8,128)}, u32[]{:S(2)}, u32[]{:S(2)}) async-start(f32[4,32,64,256]{3,2,1,0:T(8,128)} %pad_maximum_fusion.9), calls=%async_computation | async-start | bytes 16777216 | tf_op jit(solution)/shard_map/all_to_all | solution.py:155
  245.2 3.4 copy-start.1
  264.7 192.6 %all-to-all-start.1 = ((f32[32,256,256]{2,0,1:T(8,128)}), f32[32,256,256]{2,0,1:T(8,128)}, u32[]{:S(2)}, u32[]{:S(2)}) async-start(f32[32,256,256]{2,0,1:T(8,128)} %copy.159), calls=%async_computation.1 | async-start | bytes 16777216 | tf_op jit(solution)/shard_map/all_to_all | solution.py:161
